TPU v7x, 256 devices: a whole 4x4x8 slice. The times are simulated.
256 devices in a mesh: req: 4 (over x), blk: 64 (over z, y, core).
Axes of the slice: x: 4, y: 4, z: 8, core: 2. Of those that a mesh axis runs over, the one named last changes fastest.
Arguments:
- tokens: bfloat16 [4, 8192, 2048], P('req', 'blk'), may hold values from -6 to 6
- block_ids: int32 [4, 128], P('req', 'blk'), may hold values from 0 to 127, as said below
- lengths: int32 [4], P('req'), may hold values from 4097 to 8192, as said below
- page_table: int32 [4, 2, 128], P('req'), may hold values from 0 to 255, as said below
- qkv_weight: bfloat16 [2048, 3072], P(('req', 'blk')), may hold values from -0.125 to 0.125
- q_gain: float32 [256], replicated
- k_gain: float32 [256], replicated
Outputs:
- attended: bfloat16 [4, 8192, 2048], P('req', 'blk')
- kv_cache: bfloat16 [4, 256, 64, 512], P('req', 'blk')
Inputs may be any that keep to these rules, and one draw needn't show every extreme that they name: `lengths`: one prompt has length exactly 8192. `block_ids`: the two entries of one device are b and 127 - b; over a prompt the first entries are a permutation of 0 to 63. `page_table`: each prompt's entries are a permutation of 0 to 255.
All inputs are finite; a program needn't handle non-finite values.
Results may differ from a plain program's by a relative error of at most 0.013.
The roundings to bfloat16 on the way count: a program that leaves them out, or rounds other values in their place, can miss the bound.
Values may be sent and summed in bfloat16 or wider, within the bound.
A program may use at most 128 MiB of HBM per device.

v0:
```python
import math
import jax
import jax.numpy as jnp
from jax import lax
from jax.sharding import PartitionSpec as P

H = 8
KVH = 2
HD = 256
ROPE_BASE = 1000000.0
NORM_EPS = 1e-06
FLOOR_SCORE = -1e30


def head_norm(tensor, scale_gain):
    return (
        tensor
        * lax.rsqrt(jnp.mean(tensor * tensor, axis=-1, keepdims=True) + NORM_EPS)
        * scale_gain
    )


def rotary(tensor, positions):
    half_dim = tensor.shape[-1] // 2
    channel = jnp.arange(half_dim).astype(jnp.float32)
    inverse = jnp.power(jnp.float32(ROPE_BASE), -2.0 * channel / tensor.shape[-1])
    angles = positions.astype(jnp.float32)[:, None] * inverse[None, :]
    cosine = jnp.cos(angles)[:, None, :]
    sine_part = jnp.sin(angles)[:, None, :]
    front_half = tensor[..., :half_dim]
    second = tensor[..., half_dim:]
    return jnp.concatenate(
        [front_half * cosine - second * sine_part, second * cosine + front_half * sine_part], -1
    )


def body(tokens, block_ids, lengths, page_table, qkv_weight, q_gain, k_gain):
    local_rows = tokens[0]
    row_count = local_rows.shape[0]
    blk_rows = row_count // 2
    groups = H // KVH
    projected = jnp.dot(
        local_rows,
        lax.all_gather(qkv_weight, ("req", "blk"), axis=0, tiled=True),
        preferred_element_type=jnp.float32,
    )
    own_ids = block_ids[0]
    positions = (
        own_ids[:, None] * blk_rows + jnp.arange(blk_rows, dtype=jnp.int32)[None, :]
    ).reshape(row_count)
    length = lengths[0]
    query_raw = projected[:, : H * HD].reshape(row_count, H, HD)
    key_raw = projected[:, H * HD : (H + KVH) * HD].reshape(row_count, KVH, HD)
    value_raw = projected[:, (H + KVH) * HD :].reshape(row_count, KVH, HD)
    queries = (
        rotary(head_norm(query_raw, q_gain), positions)
        .astype(jnp.bfloat16)
        .reshape(row_count, KVH, groups, HD)
    )
    send_keys = (
        rotary(head_norm(key_raw, k_gain), positions)
        .astype(jnp.bfloat16)
        .reshape(row_count, KVH * HD)
    )
    send_values = head_norm(value_raw, 1.0).astype(jnp.bfloat16).reshape(row_count, KVH * HD)
    all_ids = lax.all_gather(block_ids, "blk", axis=1, tiled=True)[0]
    table_size = all_ids.shape[0]
    slot_count = page_table.shape[1] * page_table.shape[2] // lax.axis_size("blk")
    my_slots = lax.axis_index("blk") * slot_count + jnp.arange(slot_count, dtype=jnp.int32)
    slot_match = page_table[0][None, :, :] == my_slots[:, None, None]
    head_grid = jnp.arange(page_table.shape[1], dtype=jnp.int32)[None, :, None]
    block_grid = jnp.arange(page_table.shape[2], dtype=jnp.int32)[None, None, :]
    slot_head = jnp.sum(jnp.where(slot_match, head_grid, 0), axis=(1, 2))
    slot_block = jnp.sum(jnp.where(slot_match, block_grid, 0), axis=(1, 2))
    query_live = positions < length
    running_max = jnp.full((row_count, KVH, groups), FLOOR_SCORE, jnp.float32)
    running_sum = jnp.zeros((row_count, KVH, groups), jnp.float32)
    weighted = jnp.zeros((row_count, KVH, groups, HD), jnp.float32)
    pages_out = jnp.zeros((slot_count, blk_rows, 2 * HD), jnp.bfloat16)
    piece_keys = lax.all_gather(send_keys, "blk", axis=0, tiled=True)
    piece_values = lax.all_gather(send_values, "blk", axis=0, tiled=True)
    piece_rows = piece_keys.shape[0]
    global_rows = jnp.arange(piece_rows, dtype=jnp.int32)
    block_index = global_rows // blk_rows
    lookup = jnp.sum(
        jnp.where(
            block_index[:, None] == jnp.arange(table_size, dtype=jnp.int32)[None, :],
            all_ids[None, :],
            0,
        ),
        1,
    )
    key_pos = lookup * blk_rows + global_rows % blk_rows
    key_heads = piece_keys.reshape(piece_rows, KVH, HD)
    value_heads = piece_values.reshape(piece_rows, KVH, HD)
    key_block = math.gcd(piece_rows, 512)

    def one_block(block_number, running):
        block_keys = lax.dynamic_slice_in_dim(key_heads, block_number * key_block, key_block, 0)
        block_values = lax.dynamic_slice_in_dim(value_heads, block_number * key_block, key_block, 0)
        block_pos = lax.dynamic_slice_in_dim(key_pos, block_number * key_block, key_block, 0)
        allowed = (block_pos[None, :] <= positions[:, None]) & (block_pos[None, :] < length)
        old_max, old_sum, old_weighted = running
        scores = jnp.einsum(
            "rgad,kgd->rgak", queries, block_keys, preferred_element_type=jnp.float32
        )
        mask_full = allowed[:, None, None, :]
        new_max = jnp.maximum(old_max, jnp.max(jnp.where(mask_full, scores, FLOOR_SCORE), -1))
        rescale = jnp.exp(old_max - new_max)
        weights = jnp.where(mask_full, jnp.exp(scores - new_max[..., None]), 0.0)
        new_sum = old_sum * rescale + jnp.sum(weights, -1)
        product = jnp.einsum(
            "rgak,kgd->rgad",
            weights.astype(jnp.bfloat16),
            block_values,
            preferred_element_type=jnp.float32,
        )
        return (new_max, new_sum, old_weighted * rescale[..., None] + product)

    running_max, running_sum, weighted = lax.fori_loop(
        0, piece_rows // key_block, one_block, (running_max, running_sum, weighted)
    )
    paired = jnp.concatenate([key_heads, value_heads], -1)
    row_numbers = jnp.arange(piece_rows, dtype=jnp.int32)
    page_offsets = jnp.arange(blk_rows, dtype=jnp.int32)
    page_list = []
    for slot_number in range(slot_count):
        target = slot_block[slot_number] * blk_rows
        is_start = key_pos == target
        present = jnp.any(is_start)
        first_row = jnp.sum(jnp.where(is_start, row_numbers, 0))
        rows_here = lax.dynamic_slice_in_dim(paired, first_row, blk_rows, 0)
        chosen = lax.dynamic_index_in_dim(rows_here, slot_head[slot_number], 1, keepdims=False)
        live_rows = target + page_offsets < length
        chosen = jnp.where(live_rows[:, None], chosen, jnp.zeros_like(chosen))
        page_list.append(jnp.where(present, chosen, pages_out[slot_number]))
    running_max, running_sum, weighted, pages_out = (
        running_max,
        running_sum,
        weighted,
        jnp.stack(page_list),
    )
    divisor = jnp.where(query_live[:, None, None], running_sum, 1.0)
    attended = jnp.where(query_live[:, None, None, None], weighted / divisor[..., None], 0.0)
    attended = attended.reshape(row_count, H * HD).astype(jnp.bfloat16)
    return (attended[None], pages_out[None])


def solution(mesh):
    in_specs = (
        P("req", "blk", None),
        P("req", "blk"),
        P("req"),
        P("req", None, None),
        P(("req", "blk"), None),
        P(),
        P(),
    )
    out_specs = (P("req", "blk", None), P("req", "blk", None, None))
    return jax.shard_map(body, mesh=mesh, in_specs=in_specs, out_specs=out_specs, check_vma=False)
```

profile of v0, /device:TPU:1, one launch (start us, length us, event | category | flops | bytes accessed | tf_op | source)
XLA Modules:
  0.0 402.0 jit_solution(17340536434207153513)
XLA Ops:
  8.0 128.9 %all-gather.4.cloned.1.call-done = bf16[2048,3072]{1,0:T(8,128)(2,1)} async-done(((bf16[8,3072]{1,0:T(8,128)(2,1)}), bf16[2048,3072]{1,0:T(8,128)(2,1)}) %all-gather.4.cloned.1.call-update) | async-done | bytes 12582928 | tf_op jit(solution)/shard_map/all_gather | solution.py:44
  136.8 6.4 %fusion.21 = f32[128,3072]{1,0:T(8,128)S(1)} fusion(bf16[2048,3072]{1,0:T(8,128)(2,1)} %all-gather.4.cloned.1.call-done, bf16[1,128,2048]{2,1,0:T(8,128)(2,1)S(1)} %copy-done), kind=kOutput, calls=%fused_computation.43 | convolution fusion | flops 1610612736 | bytes 14680064 | tf_op jit(solution)/shard_map/dot_general | solution.py:42
  157.0 16.9 %all-reduce = s32[128]{0:T(128)S(1)} all-reduce(s32[128]{0:T(128)S(1)} %bitcast_dynamic-update-slice_fusion), channel_id=1, replica_groups=mesh['req'=4,'blk'=64] {'blk'}, use_global_device_ids=true, to_apply=%add | all-reduce | flops 128 | bytes 1024
  173.9 2.5 select_reduce_fusion
  192.6 32.3 %all-gather.8.cloned.1.call-done = bf16[8192,512]{1,0:T(8,128)(2,1)} async-done(((bf16[128,512]{1,0:T(8,128)(2,1)}), bf16[8192,512]{1,0:T(8,128)(2,1)}) %all-gather.8.cloned.1.call-update) | async-done | bytes 8388624 | tf_op jit(solution)/shard_map/all_gather | solution.py:81
  224.9 11.3 %copy.84 = bf16[8192,512]{0,1:T(8,128)(2,1)} copy(bf16[8192,512]{1,0:T(8,128)(2,1)} %all-gather.8.cloned.1.call-done) | data formatting | bytes 16777216
  236.2 74.7 %all-gather.6.cloned.1.call-done = bf16[8192,512]{0,1:T(8,128)(2,1)} async-done(((bf16[128,512]{0,1:T(8,128)(2,1)}), bf16[8192,512]{0,1:T(8,128)(2,1)}) %all-gather.6.cloned.1.call-update) | async-done | bytes 8388624 | tf_op jit(solution)/shard_map/all_gather | solution.py:80
  313.0 77.7 %while.18 = (s32[]{:T(128)}, f32[128,2,4]{0,2,1:T(4,128)S(1)}, f32[128,2,4]{0,2,1:T(4,128)S(1)}, f32[128,2,4,256]{0,3,2,1:T(8,128)S(1)}, s32[8192]{0:T(1024)S(1)...) while((s32[]{:T(128)}, f32[128,2,4]{0,2,1:T(4,128)S(1)}, ...), condition=%wide.region_7.8_spmd.clone, body=%wide.region_4.0_spmd.clone.sunk | while | flops 541988480 | bytes 10298591 | solution.py:120
  316.1 1.7 fusion.65
  321.0 1.7 fusion.65
  325.9 1.7 fusion.65
  330.7 1.7 fusion.65
  335.6 1.7 fusion.65
  340.4 1.7 fusion.65
  345.3 1.7 fusion.65
  350.2 1.7 fusion.65
  355.0 1.7 fusion.65
  359.9 1.7 fusion.65
  364.7 1.7 fusion.65
  369.6 1.7 fusion.65
  374.5 1.7 fusion.65
  379.3 1.7 fusion.65
  384.2 1.7 fusion.65
  389.0 1.7 fusion.65
  (227 shorter events, 67.6 us)
Async XLA Ops:
  7.2 129.7 %copy-start = (bf16[1,128,2048]{2,1,0:T(8,128)(2,1)S(1)}, bf16[1,128,2048]{2,1,0:T(8,128)(2,1)}, u32[]{:S(2)}) copy-start(bf16[1,128,2048]{2,1,0:T(8,128)(2,1)} %param.9) | copy-start | bytes 1572868
  7.2 129.6 %all-gather.4.cloned.1.call-start = ((), (), s32[]{:S(2)}) async-start(), calls=%async_computation | async-start | bytes 12632064 | tf_op jit(solution)/shard_map/all_gather | solution.py:44
  7.9 136.8 %copy-start.4 = (s32[1,2]{1,0:T(1,128)S(1)}, s32[1,2]{1,0:T(1,128)}, u32[]{:S(2)}) copy-start(s32[1,2]{1,0:T(1,128)} %param.10) | copy-start | bytes 28
  7.9 217.0 %all-gather.8.cloned.1.call-start = ((), (), s32[]{:S(2)}) async-start(), calls=%async_computation.2 | async-start | bytes 8519680 | tf_op jit(solution)/shard_map/all_gather | solution.py:81
  143.2 2.4 copy-start.1
  143.2 3.8 copy-start.3
  143.2 12.3 %copy-start.5 = (u32[256]{0:T(256)S(1)}, u32[256]{0:T(256)}, u32[]{:S(2)}) copy-start(u32[256]{0:T(256)} %constant.200) | copy-start | bytes 3076
  144.6 166.2 %all-gather.6.cloned.1.call-start = ((), (), s32[]{:S(2)}) async-start(), calls=%async_computation.1 | async-start | bytes 8519680 | tf_op jit(solution)/shard_map/all_gather | solution.py:80
  145.4 46.7 %copy-start.2 = (f32[256]{0:T(256)S(1)}, f32[256]{0:T(256)}, u32[]{:S(2)}) copy-start(f32[256]{0:T(256)} %param.14) | copy-start | bytes 3076
Sparse Core Ops, SparseCore 0:
  11.9 124.9 all-gather.3
  144.8 80.1 all-gather.7
  228.2 82.6 all-gather.5
where the time goes:
time: 404 us; the launch traced here: 402 us
  waiting for transfers between devices  237 us (59%)
  matrix products  59.4 us (15%)
  other arithmetic  37.3 us (9%)
  between operations  33 us (8%)
  local copies, waits for them, and re-layouts  17.7 us (4%)
  blocking collectives  16.9 us (4%)
    all_gather x1, waiting for transfers between devices, body(): lax.all_gather(qkv_weight, ('req', 'blk'), axis=0, tiled=True)  129 us
    all_gather x1, waiting for transfers between devices, body(): piece_keys = lax.all_gather(send_keys, 'blk', axis=0, tiled=True)  74.7 us
    all_gather x1, waiting for transfers between devices, body(): piece_values = lax.all_gather(send_values, 'blk', axis=0, tiled=True)  32.3 us
    dot_general x16, matrix products, one_block(): jnp.einsum('rgak,kgd->rgad', weights.astype(jnp.bfloat16), block_values,...  27.5 us
    dot_general x16, matrix products, one_block(): jnp.einsum('rgad,kgd->rgak', queries, block_keys, preferred_element_type=...  25.5 us
    unnamed x1, blocking collectives  16.9 us
    unnamed x18, local copies, waits for them, and re-layouts  12.4 us
    lt x16, other arithmetic, one_block(): block_pos[None, :] < length  11.6 us
  transfers between devices with their start and end apart: 3, of which 3 were waited for; matrix products, arithmetic and copies ran while one was open for 6% of the time, Pallas kernels for 0%

commit v1 on v0

--- a/solution.py
+++ b/solution.py
@@ -78,7 +78,10 @@
     weighted = jnp.zeros((row_count, KVH, groups, HD), jnp.float32)
     pages_out = jnp.zeros((slot_count, blk_rows, 2 * HD), jnp.bfloat16)
     piece_keys = lax.all_gather(send_keys, "blk", axis=0, tiled=True)
-    piece_values = lax.all_gather(send_values, "blk", axis=0, tiled=True)
+    count = lax.axis_size("blk")
+    shards = jnp.stack([send_values for _ in range(count)])
+    shards = lax.all_to_all(shards, "blk", split_axis=0, concat_axis=0)
+    piece_values = jnp.concatenate(shards, axis=0)
     piece_rows = piece_keys.shape[0]
     global_rows = jnp.arange(piece_rows, dtype=jnp.int32)
     block_index = global_rows // blk_rows

time: 404 us -> 510 us (1.26)
  blocking collectives: 16.9 us -> 202 us
  waiting for transfers between devices: 237 us -> 128 us
  local copies, waits for them, and re-layouts: 17.7 us -> 37 us
  starting transfers between devices: 0.12 us -> 8.05 us
    unnamed x1, blocking collectives: 16.9 us -> 202 us
    all_gather x1, waiting for transfers between devices: 74.7 us -> 0.01 us  [body(): piece_keys = lax.all_gather(send_keys, 'blk', axis=0, tiled=True)]
    all_gather x1 -> x0, waiting for transfers between devices: 32.3 us -> none  [body(): piece_values = lax.all_gather(send_values, 'blk', axis=0, tiled=True)]
    another operation x2 -> x4, local copies, waits for them, and re-layouts: 0.07 us -> 18.6 us  [the longest x1 13.3 us: body(): value_heads = piece_values.reshape(piece_rows, KVH, HD)]
    all_to_all x0 -> x1, local copies, waits for them, and re-layouts: none -> 12 us  [body(): shards = lax.all_to_all(shards, 'blk', split_axis=0, concat_axis=0)]
    unnamed x18 -> x19, local copies, waits for them, and re-layouts: 12.4 us -> 1.08 us
    all_to_all x0 -> x1, starting transfers between devices: none -> 7.97 us  [body(): shards = lax.all_to_all(shards, 'blk', split_axis=0, concat_axis=0)]
  transfers between devices with their start and end apart: 3 -> 3, of which waited for: 3 -> 1; matrix products, arithmetic and copies ran while one was open for 6% -> 7% of each run, Pallas kernels for 0% -> 0%
where the time goes in v1:
time: 510 us; the launch traced here: 506 us
  blocking collectives  202 us (40%)
  waiting for transfers between devices  128 us (25%)
  matrix products  59.4 us (12%)
  other arithmetic  37.2 us (7%)
  local copies, waits for them, and re-layouts  37 us (7%)
  between operations  32.7 us (6%)
  starting transfers between devices  8.05 us (2%)
    unnamed x1, blocking collectives  202 us
    all_gather x1, waiting for transfers between devices, body(): lax.all_gather(qkv_weight, ('req', 'blk'), axis=0, tiled=True)  128 us
    dot_general x16, matrix products, one_block(): jnp.einsum('rgak,kgd->rgad', weights.astype(jnp.bfloat16), block_values,...  27.5 us
    dot_general x16, matrix products, one_block(): jnp.einsum('rgad,kgd->rgak', queries, block_keys, preferred_element_type=...  25.5 us
    another operation x1, local copies, waits for them, and re-layouts, body(): value_heads = piece_values.reshape(piece_rows, KVH, HD)  13.3 us
    all_to_all x1, local copies, waits for them, and re-layouts, body(): shards = lax.all_to_all(shards, 'blk', split_axis=0, concat_axis=0)  12 us
    lt x16, other arithmetic, one_block(): block_pos[None, :] < length  11.6 us
  transfers between devices with their start and end apart: 3, of which 1 were waited for; matrix products, arithmetic and copies ran while one was open for 7% of the time, Pallas kernels for 0%

profile of v1, /device:TPU:1, one launch (start us, length us, event | category | flops | bytes accessed | tf_op | source)
XLA Modules:
  0.0 505.9 jit_solution(5516919232190737044)
XLA Ops:
  9.1 127.8 %all-gather.3.cloned.1.call-done = bf16[2048,3072]{1,0:T(8,128)(2,1)} async-done(((bf16[8,3072]{1,0:T(8,128)(2,1)}), bf16[2048,3072]{1,0:T(8,128)(2,1)}) %all-gather.3.cloned.1.call-update) | async-done | bytes 12582928 | tf_op jit(solution)/shard_map/all_gather | solution.py:44
  136.8 6.4 %fusion.21 = f32[128,3072]{1,0:T(8,128)S(1)} fusion(bf16[2048,3072]{1,0:T(8,128)(2,1)} %all-gather.3.cloned.1.call-done, bf16[1,128,2048]{2,1,0:T(8,128)(2,1)S(1)} %copy-done), kind=kOutput, calls=%fused_computation.43 | convolution fusion | flops 1610612736 | bytes 14680064 | tf_op jit(solution)/shard_map/dot_general | solution.py:42
  144.5 5.2 %stack.4 = bf16[64,128,512]{1,2,0:T(8,128)(2,1)} broadcast(bf16[128,512]{0,1:T(8,128)(2,1)S(1)} %copy.86), dimensions={1,2} | broadcast | bytes 8519680 | tf_op jit(solution)/shard_map/stack | solution.py:82
  149.7 8.0 %all-to-all-start = ((bf16[64,128,512]{1,2,0:T(8,128)(2,1)}), bf16[64,128,512]{1,2,0:T(8,128)(2,1)}, u32[]{:S(2)}, u32[]{:S(2)}) async-start(bf16[64,128,512]{1,2,0:T(8,128)(2,1)} %stack.4), calls=%async_computation | async-start | bytes 16777216 | tf_op jit(solution)/shard_map/all_to_all | solution.py:83
  168.8 202.1 %all-reduce = s32[128]{0:T(128)S(1)} all-reduce(s32[128]{0:T(128)S(1)} %bitcast_dynamic-update-slice_fusion), channel_id=1, replica_groups=mesh['req'=4,'blk'=64] {'blk'}, use_global_device_ids=true, to_apply=%add | all-reduce | flops 128 | bytes 1024
  370.9 2.5 select_reduce_fusion
  389.2 12.0 %copy.87 = bf16[64,128,512]{1,0,2:T(8,128)(2,1)} copy(bf16[64,128,512]{1,2,0:T(8,128)(2,1)} %all-to-all-done) | data formatting | bytes 16777216 | tf_op jit(solution)/shard_map/all_to_all | solution.py:83
  401.2 13.3 %reshape_reshape.3 = bf16[8192,2,256]{0,2,1:T(8,128)(2,1)} reshape(bf16[64,128,512]{1,0,2:T(8,128)(2,1)} %copy.87) | data formatting | bytes 16777216 | tf_op jit(solution)/shard_map/reshape;reshape | solution.py:98
  414.5 77.8 %while.18 = (s32[]{:T(128)}, f32[128,2,4]{0,2,1:T(4,128)S(1)}, f32[128,2,4]{0,2,1:T(4,128)S(1)}, f32[128,2,4,256]{0,3,2,1:T(8,128)S(1)}, s32[8192]{0:T(1024)S(1)...) while((s32[]{:T(128)}, f32[128,2,4]{0,2,1:T(4,128)S(1)}, ...), condition=%wide.region_7.8_spmd.clone, body=%wide.region_4.0_spmd.clone.sunk | while | flops 541988480 | bytes 10298591 | solution.py:123
  417.6 1.7 fusion.65
  422.5 1.7 fusion.65
  427.4 1.7 fusion.65
  432.2 1.7 fusion.65
  442.0 1.7 fusion.65
  446.8 1.7 fusion.65
  456.5 1.7 fusion.65
  461.4 1.7 fusion.65
  466.3 1.7 fusion.65
  471.1 1.7 fusion.65
  476.0 1.7 fusion.65
  480.9 1.7 fusion.65
  485.7 1.7 fusion.65
  490.6 1.7 fusion.65
  493.5 1.8 fusion.24
  (231 shorter events, 69.1 us)
Async XLA Ops:
  7.2 129.7 %copy-start = (bf16[1,128,2048]{2,1,0:T(8,128)(2,1)S(1)}, bf16[1,128,2048]{2,1,0:T(8,128)(2,1)}, u32[]{:S(2)}) copy-start(bf16[1,128,2048]{2,1,0:T(8,128)(2,1)} %param.9) | copy-start | bytes 1572868
  7.2 129.6 %all-gather.3.cloned.1.call-start = ((), (), s32[]{:S(2)}) async-start(), calls=%async_computation.1 | async-start | bytes 12632064 | tf_op jit(solution)/shard_map/all_gather | solution.py:44
  149.7 8.1 %copy-start.2 = (f32[256]{0:T(256)S(1)}, f32[256]{0:T(256)}, u32[]{:S(2)}) copy-start(f32[256]{0:T(256)} %param.15) | copy-start | bytes 3076
  149.7 9.4 %copy-start.4 = (s32[1,2,128]{2,1,0:T(2,128)S(1)}, s32[1,2,128]{2,1,0:T(2,128)}, u32[]{:S(2)}) copy-start(s32[1,2,128]{2,1,0:T(2,128)} %param.12) | copy-start | bytes 3076
  149.7 17.8 %copy-start.6 = (u32[256]{0:T(256)S(1)}, u32[256]{0:T(256)}, u32[]{:S(2)}) copy-start(u32[256]{0:T(256)} %constant.200) | copy-start | bytes 3076
  149.7 19.0 %copy-start.5 = (s32[1,2]{1,0:T(1,128)S(1)}, s32[1,2]{1,0:T(1,128)}, u32[]{:S(2)}) copy-start(s32[1,2]{1,0:T(1,128)} %param.10) | copy-start | bytes 28
  149.7 239.5 %all-to-all-start = ((bf16[64,128,512]{1,2,0:T(8,128)(2,1)}), bf16[64,128,512]{1,2,0:T(8,128)(2,1)}, u32[]{:S(2)}, u32[]{:S(2)}) async-start(bf16[64,128,512]{1,2,0:T(8,128)(2,1)} %stack.4), calls=%async_computation | async-start | bytes 16777216 | tf_op jit(solution)/shard_map/all_to_all | solution.py:83
  157.7 231.0 %copy-start.3 = (f32[256]{0:T(256)S(1)}, f32[256]{0:T(256)}, u32[]{:S(2)}) copy-start(f32[256]{0:T(256)} %param.14) | copy-start | bytes 3076
  157.7 256.8 %all-gather.5.cloned.1.call-start = ((), (), s32[]{:S(2)}) async-start(), calls=%async_computation.2 | async-start | bytes 8519680 | tf_op jit(solution)/shard_map/all_gather | solution.py:80
  493.5 5.6 %copy-start.1 = (bf16[1,128,2048]{2,1,0:T(8,128)(2,1)S(1)}, bf16[1,128,2048]{2,1,0:T(8,128)(2,1)}, u32[]{:S(2)}) copy-start(bf16[1,128,2048]{2,1,0:T(8,128)(2,1)} %param.9) | copy-start | bytes 1572868
Sparse Core Ops, SparseCore 0:
  11.9 124.9 all-gather.2
  161.8 183.5 all-gather.4
